TPU v7x, 32 devices: a whole 2x2x4 slice. The times are simulated.
32 devices in a mesh: gx: 2 (over y), gy: 4 (over x, core), gz: 4 (over z).
Axes of the slice: x: 2, y: 2, z: 4, core: 2. Of those that a mesh axis runs over, the one named last changes fastest.
Arguments:
- tokens: bfloat16 [256, 8192], P('gx', 'gy'), may hold values from -6 to 6
- cotangent: bfloat16 [256, 8192], P('gx', 'gy'), may hold values from -6 to 6
- gate_weight: bfloat16 [8192, 28672], P('gy', ('gx', 'gz')), may hold values from -5.7452426 to 5.7452426
- up_weight: bfloat16 [8192, 28672], P('gy', ('gx', 'gz')), may hold values from -5.7452426 to 5.7452426
- down_weight: bfloat16 [28672, 8192], P(('gx', 'gz'), 'gy'), may hold values from -3.0709613 to 3.0709613
- gate_reduce: bfloat16 [8192, 32], P('gy'), may hold values from -0.0625 to 0.0625
- gate_expand: bfloat16 [32, 28672], P(None, ('gx', 'gz')), may hold values from -5 to 5
- gate_magnitude: float32 [28672], P(('gx', 'gz')), may hold values from 0.5 to 2
- up_reduce: bfloat16 [8192, 32], P('gy'), may hold values from -0.0625 to 0.0625
- up_expand: bfloat16 [32, 28672], P(None, ('gx', 'gz')), may hold values from -5 to 5
- up_magnitude: float32 [28672], P(('gx', 'gz')), may hold values from 0.5 to 2
- down_reduce: bfloat16 [28672, 32], P(('gx', 'gz')), may hold values from -0.03125 to 0.03125
- down_expand: bfloat16 [32, 8192], P(None, 'gy'), may hold values from -5 to 5
- down_magnitude: float32 [8192], P('gy'), may hold values from 0.5 to 2
Outputs:
- output: bfloat16 [256, 8192], P('gx', 'gy')
- grad_tokens: bfloat16 [256, 8192], P('gx', 'gy')
- grad_gate_reduce: float32 [8192, 32], P('gy')
- grad_gate_expand: float32 [32, 28672], P(None, ('gx', 'gz'))
- grad_gate_magnitude: float32 [28672], P(('gx', 'gz'))
- grad_up_reduce: float32 [8192, 32], P('gy')
- grad_up_expand: float32 [32, 28672], P(None, ('gx', 'gz'))
- grad_up_magnitude: float32 [28672], P(('gx', 'gz'))
- grad_down_reduce: float32 [28672, 32], P(('gx', 'gz'))
- grad_down_expand: float32 [32, 8192], P(None, 'gy')
- grad_down_magnitude: float32 [8192], P('gy')
All inputs are finite; a program needn't handle non-finite values.
Results may differ from a plain program's by a relative error of at most 0.012.
Values may be sent and summed in bfloat16 or wider, within the bound.
No kernel may reach another device: no remote copies, remote signals or barrier semaphores. Data moves between devices by JAX's collectives and lax.ppermute only.
A program may use at most 128 MiB of HBM per device.

v0:
```python
import jax
import jax.numpy as jnp
from jax import lax
from jax.sharding import PartitionSpec as P

EPSILON = 1e-06


def tile_square(weight, reduce_in, expand_out):
    merged = weight.astype(jnp.float32) + jnp.dot(
        reduce_in, expand_out, preferred_element_type=jnp.float32
    )
    return jnp.sum(merged * merged, axis=0)


def share_rows(values, count):
    return lax.dynamic_slice_in_dim(values, lax.axis_index("gz") * count, count, 0)


def contract_last(left, right):
    return lax.dot_general(
        left, right, (((1,), (1,)), ((), ())), preferred_element_type=jnp.float32
    )


def contract_first(left, right):
    return lax.dot_general(
        left, right, (((0,), (0,)), ((), ())), preferred_element_type=jnp.float32
    )


def on_device(
    tokens,
    cotangent,
    gate_weight,
    up_weight,
    down_weight,
    gate_reduce,
    gate_expand,
    gate_magnitude,
    up_reduce,
    up_expand,
    up_magnitude,
    down_reduce,
    down_expand,
    down_magnitude,
):
    share_count = tokens.shape[0] // lax.axis_size("gz")
    square_gate = tile_square(gate_weight, gate_reduce, gate_expand)
    square_up = tile_square(up_weight, up_reduce, up_expand)
    square_down = tile_square(down_weight, down_reduce, down_expand)
    norm_down = jnp.sqrt(lax.psum(square_down, ("gx", "gz")) + EPSILON)
    scale_down = down_magnitude / norm_down
    all_tokens = lax.all_gather(tokens, "gx", axis=0, tiled=True)
    part_gate = jnp.dot(all_tokens, gate_weight, preferred_element_type=jnp.float32)
    part_up = jnp.dot(all_tokens, up_weight, preferred_element_type=jnp.float32)
    low_gate_part = jnp.dot(all_tokens, gate_reduce, preferred_element_type=jnp.float32)
    low_up_part = jnp.dot(all_tokens, up_reduce, preferred_element_type=jnp.float32)
    gate_lin, up_lin, gate_lowsum, up_lowsum = (
        lax.psum_scatter(part_gate, "gy", scatter_dimension=0, tiled=True),
        lax.psum_scatter(part_up, "gy", scatter_dimension=0, tiled=True),
        lax.psum_scatter(low_gate_part, "gy", scatter_dimension=0, tiled=True),
        lax.psum_scatter(low_up_part, "gy", scatter_dimension=0, tiled=True),
    )
    summed_gate, summed_up = lax.psum((square_gate, square_up), "gy")
    norm_gate = jnp.sqrt(summed_gate + EPSILON)
    norm_up = jnp.sqrt(summed_up + EPSILON)
    scale_gate = gate_magnitude / norm_gate
    scale_up = up_magnitude / norm_up
    gate_low = gate_lowsum.astype(jnp.bfloat16)
    up_low = up_lowsum.astype(jnp.bfloat16)
    gate_lin = gate_lin + jnp.dot(gate_low, gate_expand, preferred_element_type=jnp.float32)
    up_lin = up_lin + jnp.dot(up_low, up_expand, preferred_element_type=jnp.float32)
    gate_pre = gate_lin * scale_gate[None, :]
    up_pre = up_lin * scale_up[None, :]
    sigmoid_gate = jax.nn.sigmoid(gate_pre)
    active = gate_pre * sigmoid_gate
    hidden = (active * up_pre).astype(jnp.bfloat16)
    all_hidden = lax.all_gather(hidden, "gy", axis=0, tiled=True)
    part_down = jnp.dot(all_hidden, down_weight, preferred_element_type=jnp.float32)
    low_down_part = jnp.dot(all_hidden, down_reduce, preferred_element_type=jnp.float32)
    down_lin, down_lowsum = (
        lax.psum_scatter(part_down, "gx", scatter_dimension=0, tiled=True),
        lax.psum_scatter(low_down_part, "gx", scatter_dimension=0, tiled=True),
    )
    down_lin, down_lowsum = lax.psum((down_lin, down_lowsum), "gz")
    down_low = down_lowsum.astype(jnp.bfloat16)
    down_lin = down_lin + jnp.dot(down_low, down_expand, preferred_element_type=jnp.float32)
    output = (down_lin * scale_down[None, :]).astype(jnp.bfloat16)
    down_lin = share_rows(down_lin, share_count)
    down_low = share_rows(down_low, share_count)
    cot_float = cotangent.astype(jnp.float32)
    down_delta = (cot_float * scale_down[None, :]).astype(jnp.bfloat16)
    cot_share = share_rows(cot_float, share_count)
    delta_share = share_rows(down_delta, share_count)
    grad_down_magnitude = jnp.sum(cot_share * down_lin, axis=0) / norm_down
    grad_down_expand = contract_first(down_low, delta_share)
    grad_down_magnitude, grad_down_expand = lax.psum(
        (grad_down_magnitude, grad_down_expand), ("gx", "gz")
    )
    all_delta = lax.all_gather(down_delta, "gx", axis=0, tiled=True)
    part_hidden_grad = contract_last(all_delta, down_weight)
    part_down_back = contract_last(all_delta, down_expand)
    hidden_gradsum, down_backsum = (
        lax.psum_scatter(part_hidden_grad, "gy", scatter_dimension=0, tiled=True),
        lax.psum_scatter(part_down_back, "gy", scatter_dimension=0, tiled=True),
    )
    down_back = down_backsum.astype(jnp.bfloat16)
    hidden_grad = (hidden_gradsum + contract_last(down_back, down_reduce)).astype(jnp.bfloat16)
    grad_down_reduce = contract_first(hidden, down_back)
    hgrad_float = hidden_grad.astype(jnp.float32)
    gate_grad = hgrad_float * up_pre * sigmoid_gate * (1.0 + gate_pre * (1.0 - sigmoid_gate))
    up_grad = hgrad_float * active
    gate_delta = (gate_grad * scale_gate[None, :]).astype(jnp.bfloat16)
    up_delta = (up_grad * scale_up[None, :]).astype(jnp.bfloat16)
    grad_gate_magnitude = jnp.sum(gate_grad * gate_lin, axis=0) / norm_gate
    grad_up_magnitude = jnp.sum(up_grad * up_lin, axis=0) / norm_up
    grad_gate_expand = contract_first(gate_low, gate_delta)
    grad_up_expand = contract_first(up_low, up_delta)
    grad_down_reduce, grad_gate_magnitude, grad_up_magnitude, grad_gate_expand, grad_up_expand = (
        lax.psum(
            (
                grad_down_reduce,
                grad_gate_magnitude,
                grad_up_magnitude,
                grad_gate_expand,
                grad_up_expand,
            ),
            "gy",
        )
    )
    all_gate_delta, all_up_delta = (
        lax.all_gather(gate_delta, "gy", axis=0, tiled=True),
        lax.all_gather(up_delta, "gy", axis=0, tiled=True),
    )
    part_input = contract_last(all_gate_delta, gate_weight) + contract_last(all_up_delta, up_weight)
    part_gate_back = contract_last(all_gate_delta, gate_expand)
    part_up_back = contract_last(all_up_delta, up_expand)
    input_sum, gate_backsum, up_backsum = (
        lax.psum_scatter(part_input, "gx", scatter_dimension=0, tiled=True),
        lax.psum_scatter(part_gate_back, "gx", scatter_dimension=0, tiled=True),
        lax.psum_scatter(part_up_back, "gx", scatter_dimension=0, tiled=True),
    )
    input_sum, gate_backsum, up_backsum = lax.psum((input_sum, gate_backsum, up_backsum), "gz")
    gate_back = gate_backsum.astype(jnp.bfloat16)
    up_back = up_backsum.astype(jnp.bfloat16)
    grad_tokens = (
        input_sum + contract_last(gate_back, gate_reduce) + contract_last(up_back, up_reduce)
    ).astype(jnp.bfloat16)
    gate_back = share_rows(gate_back, share_count)
    up_back = share_rows(up_back, share_count)
    token_share = share_rows(tokens, share_count)
    grad_gate_reduce = contract_first(token_share, gate_back)
    grad_up_reduce = contract_first(token_share, up_back)
    grad_gate_reduce, grad_up_reduce = lax.psum((grad_gate_reduce, grad_up_reduce), ("gx", "gz"))
    return (
        output,
        grad_tokens,
        grad_gate_reduce,
        grad_gate_expand,
        grad_gate_magnitude,
        grad_up_reduce,
        grad_up_expand,
        grad_up_magnitude,
        grad_down_reduce,
        grad_down_expand,
        grad_down_magnitude,
    )


def solution(mesh):
    return jax.shard_map(
        on_device,
        mesh=mesh,
        in_specs=(
            P("gx", "gy"),
            P("gx", "gy"),
            P("gy", ("gx", "gz")),
            P("gy", ("gx", "gz")),
            P(("gx", "gz"), "gy"),
            P("gy", None),
            P(None, ("gx", "gz")),
            P(("gx", "gz")),
            P("gy", None),
            P(None, ("gx", "gz")),
            P(("gx", "gz")),
            P(("gx", "gz"), None),
            P(None, "gy"),
            P("gy"),
        ),
        out_specs=(
            P("gx", "gy"),
            P("gx", "gy"),
            P("gy", None),
            P(None, ("gx", "gz")),
            P(("gx", "gz")),
            P("gy", None),
            P(None, ("gx", "gz")),
            P(("gx", "gz")),
            P(("gx", "gz"), None),
            P(None, "gy"),
            P("gy"),
        ),
        check_vma=False,
    )
```

profile of v0, /device:TPU:0, one launch (start us, length us, event | category | flops | bytes accessed | tf_op | source)
XLA Modules:
  0.0 689.7 jit_solution(911645773237748030)
XLA Ops:
  7.3 9.5 %multiply_reduce_fusion = f32[2048]{0:T(1024)S(1)} fusion(bf16[3584,2048]{1,0:T(8,128)(2,1)} %param.18, bf16[3584,32]{0,1:T(8,128)(2,1)} %param.25, bf16[32,2048]{1,0:T(8,128)(2,1)} %param.26), kind=kOutput, calls=%fused_computation | convolution fusion | flops 499120128 | bytes 15048704 | tf_op jit(solution)/shard_map/dot_general | solution.py:10
  16.8 23.7 %psum.123 = f32[2048]{0:T(1024)S(1)} all-reduce(f32[2048]{0:T(1024)S(1)} %multiply_reduce_fusion), channel_id=1, replica_groups=mesh['gx'=2,'gy'=4,'gz'=4] {'gx','gz'}, use_global_device_ids=true, to_apply=%region_13.0 | all-reduce | flops 2048 | bytes 16384 | tf_op jit(solution)/shard_map/psum | solution.py:52
  42.3 17.9 %all-gather.10.cloned.1.call-done = bf16[256,2048]{1,0:T(8,128)(2,1)} async-done(((bf16[128,2048]{1,0:T(8,128)(2,1)}), bf16[256,2048]{1,0:T(8,128)(2,1)}) %all-gather.10.cloned.1.call-update) | async-done | bytes 1048592 | tf_op jit(solution)/shard_map/all_gather | solution.py:101
  62.6 20.5 %all-gather.6.cloned.1.call-done = bf16[256,2048]{1,0:T(8,128)(2,1)} async-done(((bf16[128,2048]{1,0:T(8,128)(2,1)}), bf16[256,2048]{1,0:T(8,128)(2,1)}) %all-gather.6.cloned.1.call-update) | async-done | bytes 1048592 | tf_op jit(solution)/shard_map/all_gather | solution.py:54
  87.8 11.4 %fusion.37 = f32[256,3584]{1,0:T(8,128)} fusion(bf16[256,2048]{1,0:T(8,128)(2,1)} %all-gather.10.cloned.1.call-done, bf16[3584,2048]{1,0:T(8,128)(2,1)} %param.18), kind=kOutput, calls=%fused_computation.60 | convolution fusion | flops 3758096384 | bytes 19398656 | tf_op jit(solution)/shard_map/dot_general | solution.py:21
  133.1 10.9 %all-reduce.4 = (f32[3584]{0:T(1024)S(1)}, f32[3584]{0:T(1024)S(1)}) all-reduce(f32[3584]{0:T(1024)S(1)} %multiply_reduce_fusion.1, f32[3584]{0:T(1024)S(1)} %multiply_reduce_fusion.2), channel_id=1, replica_groups=mesh['gx'=2,'gy'=4,'gz'=4] {'gy'}, use_global_device_ids=true, to_apply=%region_7.0 | all-reduce | flops 7168 | bytes 57344 | tf_op jit(solution)/shard_map/psum | solution.py:65
  151.6 42.8 %reduce-scatter.26.cloned.1.call-done = f32[64,3584]{1,0:T(8,128)} async-done(((f32[256,3584]{1,0:T(8,128)}), f32[64,3584]{1,0:T(8,128)}) %reduce-scatter.26.cloned.1.call-update) | async-done | bytes 917520 | tf_op jit(solution)/shard_map/reduce_scatter | solution.py:105
  195.9 42.3 %reduce-scatter.18.cloned.1.call-done = f32[64,3584]{1,0:T(8,128)} async-done(((f32[256,3584]{1,0:T(8,128)}), f32[64,3584]{1,0:T(8,128)}) %reduce-scatter.18.cloned.1.call-update) | async-done | bytes 917520 | tf_op jit(solution)/shard_map/reduce_scatter | solution.py:60
  239.7 42.3 %reduce-scatter.20.cloned.1.call-done = f32[64,3584]{1,0:T(8,128)} async-done(((f32[256,3584]{1,0:T(8,128)}), f32[64,3584]{1,0:T(8,128)}) %reduce-scatter.20.cloned.1.call-update) | async-done | bytes 917520 | tf_op jit(solution)/shard_map/reduce_scatter | solution.py:61
  288.0 19.6 %all-gather.12.cloned.1.call-done = bf16[256,3584]{1,0:T(8,128)(2,1)} async-done(((bf16[64,3584]{1,0:T(8,128)(2,1)}), bf16[256,3584]{1,0:T(8,128)(2,1)}) %all-gather.12.cloned.1.call-update) | async-done | bytes 1835024 | tf_op jit(solution)/shard_map/all_gather | solution.py:133
  307.7 11.0 %fusion.39 = f32[256,2048]{1,0:T(8,128)} fusion(bf16[256,3584]{1,0:T(8,128)(2,1)} %all-gather.12.cloned.1.call-done, bf16[2048,3584]{1,0:T(8,128)(2,1)} %param.16), kind=kOutput, calls=%fused_computation.62 | convolution fusion | flops 3758096384 | bytes 18612224 | tf_op jit(solution)/shard_map/dot_general | solution.py:21
  318.7 12.1 %all-gather.14.cloned.1.call-done = bf16[256,3584]{1,0:T(8,128)(2,1)} async-done(((bf16[64,3584]{1,0:T(8,128)(2,1)}), bf16[256,3584]{1,0:T(8,128)(2,1)}) %all-gather.14.cloned.1.call-update) | async-done | bytes 1835024 | tf_op jit(solution)/shard_map/all_gather | solution.py:134
  330.8 11.6 %convolution_add_fusion.3 = f32[256,2048]{1,0:T(8,128)} fusion(f32[256,2048]{1,0:T(8,128)} %fusion.39, bf16[256,3584]{1,0:T(8,128)(2,1)} %all-gather.14.cloned.1.call-done, bf16[2048,3584]{1,0:T(8,128)(2,1)} %param.17), kind=kOutput, calls=%fused_computation.8 | convolution fusion | flops 3758620672 | bytes 20709376 | tf_op jit(solution)/shard_map/dot_general | solution.py:21
  342.5 11.6 %all-gather.8.cloned.1.call-done = bf16[256,3584]{1,0:T(8,128)(2,1)} async-done(((bf16[64,3584]{1,0:T(8,128)(2,1)}), bf16[256,3584]{1,0:T(8,128)(2,1)}) %all-gather.8.cloned.1.call-update) | async-done | bytes 1835024 | tf_op jit(solution)/shard_map/all_gather | solution.py:79
  354.1 11.0 %fusion.35 = f32[256,2048]{1,0:T(8,128)} fusion(bf16[256,3584]{1,0:T(8,128)(2,1)} %all-gather.8.cloned.1.call-done, bf16[3584,2048]{1,0:T(8,128)(2,1)} %param.18), kind=kOutput, calls=%fused_computation.58 | convolution fusion | flops 3758096384 | bytes 18612224 | tf_op jit(solution)/shard_map/dot_general | solution.py:80
  373.7 14.4 %reduce-scatter.28.cloned.1.call-done = f32[128,2048]{1,0:T(8,128)} async-done(((f32[256,2048]{1,0:T(8,128)}), f32[128,2048]{1,0:T(8,128)}) %reduce-scatter.28.cloned.1.call-update) | async-done | bytes 1048592 | tf_op jit(solution)/shard_map/reduce_scatter | solution.py:140
  388.1 34.2 %reduce-scatter.22.cloned.1.call-done = f32[128,2048]{1,0:T(8,128)} async-done(((f32[256,2048]{1,0:T(8,128)}), f32[128,2048]{1,0:T(8,128)}) %reduce-scatter.22.cloned.1.call-update) | async-done | bytes 1048592 | tf_op jit(solution)/shard_map/reduce_scatter | solution.py:83
  427.0 11.5 %all-reduce.3 = (f32[3584]{0:T(1024)}, f32[3584]{0:T(1024)}) all-reduce(f32[3584]{0:T(1024)S(1)} %get-tuple-element.33, f32[3584]{0:T(1024)S(1)} %get-tuple-element.34), channel_id=1, replica_groups=mesh['gx'=2,'gy'=4,'gz'=4] {'gy'}, use_global_device_ids=true, to_apply=%region_25.0 | all-reduce | flops 7168 | bytes 57344 | tf_op jit(solution)/shard_map/psum | solution.py:121
  447.5 12.6 %reduce-scatter.32.cloned.1.call-done = f32[128,32]{0,1:T(8,128)} async-done(((f32[256,32]{0,1:T(8,128)}), f32[128,32]{0,1:T(8,128)}) %reduce-scatter.32.cloned.1.call-update) | async-done | bytes 16400 | tf_op jit(solution)/shard_map/reduce_scatter | solution.py:142
  460.1 21.1 %all-reduce.1 = (bf16[128,32]{0,1:T(8,128)(2,1)S(1)}, bf16[128,32]{0,1:T(8,128)(2,1)S(1)}, bf16[128,32]{0,1:T(8,128)(2,1)S(1)}) all-reduce(f32[128,32]{0,1:T(8,128)} %reduce-scatter.24.cloned.1.call-done, f32[128,32]{0,1:T(8,128)} %reduce-scatter.30.cloned.1.call-done, ...), channel_id=1, replica_groups=mesh['gx'=2,'gy'=4,'gz'=4] {'gz'}, use_global_device_ids=true, to_apply=%region_11.0 | all-reduce | flops 12288 | bytes 73728 | tf_op jit(solution)/shard_map/psum | solution.py:86
  485.0 64.4 %all-reduce.12.cloned.1.call-done = (f32[128,2048]{1,0:T(8,128)}, f32[128,2048]{1,0:T(8,128)}) async-done(((f32[128,2048]{1,0:T(8,128)}, f32[128,2048]{1,0:T(8,128)}), (f32[128,2048]{1,0:T(8,128)}, f32[128,2048]{1,0:T(8,128)})) %all-reduce.12.cloned.1.call-update) | async-done | bytes 2097168 | tf_op jit(solution)/shard_map/psum | solution.py:86
  551.8 20.5 %psum.135 = f32[2048]{0:T(1024)} all-reduce(f32[2048]{0:T(1024)S(1)} %fusion.17), channel_id=1, replica_groups=mesh['gx'=2,'gy'=4,'gz'=4] {'gx','gz'}, use_global_device_ids=true, to_apply=%region_33.0 | all-reduce | flops 2048 | bytes 16384 | tf_op jit(solution)/shard_map/psum | solution.py:98
  574.9 17.2 %all-reduce.14.cloned.1.call-done = (f32[32,3584]{1,0:T(8,128)}, f32[32,3584]{1,0:T(8,128)}, f32[3584,32]{0,1:T(8,128)}) async-done(((f32[32,3584]{1,0:T(8,128)}, f32[32,3584]{1,0:T(8,128)}, f32[3584,32]{0,1:T(8,128)}), (f32[32,3584]{1,0:T(8,128)}, f32[32,3584]{1,0:T(8,128)}, f32[3584,32]{0,1:T(8,128)})) %all-reduce.14.cloned.1.call-update) | async-done | bytes 1376272 | tf_op jit(solution)/shard_map/psum | solution.py:121
  592.1 80.6 %all-reduce.10.cloned.1.call-done = (f32[2048,32]{0,1:T(8,128)}, f32[2048,32]{0,1:T(8,128)}, f32[32,2048]{1,0:T(8,128)}) async-done(((f32[2048,32]{0,1:T(8,128)}, f32[2048,32]{0,1:T(8,128)}, f32[32,2048]{1,0:T(8,128)}), (f32[2048,32]{0,1:T(8,128)}, f32[2048,32]{0,1:T(8,128)}, f32[32,2048]{1,0:T(8,128)})) %all-reduce.10.cloned.1.call-update) | async-done | bytes 786448 | tf_op jit(solution)/shard_map/psum | solution.py:155
  (117 shorter events, 100.6 us)
Async XLA Ops:
  7.2 110.7 %copy-start = (bf16[32,3584]{1,0:T(8,128)(2,1)S(1)}, bf16[32,3584]{1,0:T(8,128)(2,1)}, u32[]{:S(2)}) copy-start(bf16[32,3584]{1,0:T(8,128)(2,1)} %param.23) | copy-start | bytes 688132
  7.2 52.9 %all-gather.10.cloned.1.call-start = ((), (), s32[]{:S(2)}) async-start(), calls=%async_computation.17 | async-start | bytes 1572864 | tf_op jit(solution)/shard_map/all_gather | solution.py:101
  41.5 41.5 %all-gather.6.cloned.1.call-start = ((), (), s32[]{:S(2)}) async-start(), calls=%async_computation.11 | async-start | bytes 1572864 | tf_op jit(solution)/shard_map/all_gather | solution.py:54
  42.2 102.3 %reduce-scatter.38.cloned.1.call-start = ((), (), s32[]{:S(2)}) async-start(), calls=%async_computation.26 | async-start | bytes 163840
  62.5 82.9 %reduce-scatter.34.cloned.1.call-start = ((), (), s32[]{:S(2)}) async-start(), calls=%async_computation.24 | async-start | bytes 163840
  85.4 65.4 %reduce-scatter.36.cloned.1.call-start = ((), (), s32[]{:S(2)}) async-start(), calls=%async_computation.25 | async-start | bytes 163840
  87.8 106.7 %reduce-scatter.26.cloned.1.call-start = ((), (), s32[]{:S(2)}) async-start(), calls=%async_computation.18 | async-start | bytes 4587520 | tf_op jit(solution)/shard_map/reduce_scatter | solution.py:105
  99.2 139.0 %reduce-scatter.18.cloned.1.call-start = ((), (), s32[]{:S(2)}) async-start(), calls=%async_computation.12 | async-start | bytes 4587520 | tf_op jit(solution)/shard_map/reduce_scatter | solution.py:60
  108.4 173.6 %reduce-scatter.20.cloned.1.call-start = ((), (), s32[]{:S(2)}) async-start(), calls=%async_computation.13 | async-start | bytes 4587520 | tf_op jit(solution)/shard_map/reduce_scatter | solution.py:61
  117.9 189.8 %all-gather.12.cloned.1.call-start = ((), (), s32[]{:S(2)}) async-start(), calls=%async_computation.19 | async-start | bytes 2293760 | tf_op jit(solution)/shard_map/all_gather | solution.py:133
  151.6 167.1 %copy-start.13 = (bf16[64,32]{0,1:T(8,128)(2,1)}, bf16[64,32]{0,1:T(8,128)(2,1)S(1)}, u32[]{:S(2)}) copy-start(bf16[64,32]{0,1:T(8,128)(2,1)S(1)} %copy.28) | copy-start | bytes 12292
  286.5 44.4 %all-gather.14.cloned.1.call-start = ((), (), s32[]{:S(2)}) async-start(), calls=%async_computation.20 | async-start | bytes 2293760 | tf_op jit(solution)/shard_map/all_gather | solution.py:134
  287.0 67.0 %all-gather.8.cloned.1.call-start = ((), (), s32[]{:S(2)}) async-start(), calls=%async_computation.14 | async-start | bytes 2293760 | tf_op jit(solution)/shard_map/all_gather | solution.py:79
  287.8 100.3 %reduce-scatter.28.cloned.1.call-start = ((), (), s32[]{:S(2)}) async-start(), calls=%async_computation.21 | async-start | bytes 3145728 | tf_op jit(solution)/shard_map/reduce_scatter | solution.py:140
  342.4 80.9 %copy-start.5 = (bf16[64,3584]{1,0:T(8,128)(2,1)S(1)}, bf16[64,3584]{1,0:T(8,128)(2,1)}, u32[]{:S(2)}) copy-start(bf16[64,3584]{1,0:T(8,128)(2,1)} %get-tuple-element.30) | copy-start | bytes 1376260
  342.4 81.9 %copy-start.4 = (bf16[64,3584]{1,0:T(8,128)(2,1)S(1)}, bf16[64,3584]{1,0:T(8,128)(2,1)}, u32[]{:S(2)}) copy-start(bf16[64,3584]{1,0:T(8,128)(2,1)} %get-tuple-element.29) | copy-start | bytes 1376260
  342.5 79.8 %reduce-scatter.22.cloned.1.call-start = ((), (), s32[]{:S(2)}) async-start(), calls=%async_computation.15 | async-start | bytes 3145728 | tf_op jit(solution)/shard_map/reduce_scatter | solution.py:83
  365.1 118.0 %copy-start.6 = (bf16[128,2048]{1,0:T(8,128)(2,1)S(1)}, bf16[128,2048]{1,0:T(8,128)(2,1)}, u32[]{:S(2)}) copy-start(bf16[128,2048]{1,0:T(8,128)(2,1)} %param.14) | copy-start | bytes 1572868
  365.1 73.3 %reduce-scatter.30.cloned.1.call-start = ((), (), s32[]{:S(2)}) async-start(), calls=%async_computation.22 | async-start | bytes 49152 | tf_op jit(solution)/shard_map/reduce_scatter | solution.py:141
  368.0 79.5 %reduce-scatter.24.cloned.1.call-start = ((), (), s32[]{:S(2)}) async-start(), calls=%async_computation.16 | async-start | bytes 49152 | tf_op jit(solution)/shard_map/reduce_scatter | solution.py:84
  370.8 89.3 %reduce-scatter.32.cloned.1.call-start = ((), (), s32[]{:S(2)}) async-start(), calls=%async_computation.23 | async-start | bytes 49152 | tf_op jit(solution)/shard_map/reduce_scatter | solution.py:142
  373.7 175.7 %all-reduce.12.cloned.1.call-start = ((), (), s32[]{:S(2)}) async-start(), calls=%async_computation.28 | async-start | bytes 4194304 | tf_op jit(solution)/shard_map/psum | solution.py:86
  422.3 169.8 %all-reduce.14.cloned.1.call-start = ((), (), s32[]{:S(2)}) async-start(), calls=%async_computation.29 | async-start | bytes 2752512 | tf_op jit(solution)/shard_map/psum | solution.py:121
  426.0 246.7 %all-reduce.10.cloned.1.call-start = ((), (), s32[]{:S(2)}) async-start(), calls=%async_computation.27 | async-start | bytes 1572864 | tf_op jit(solution)/shard_map/psum | solution.py:155
  (12 other events, 479.4 us)
Sparse Core Ops, SparseCore 0:
  41.6 18.5 all-gather.9
  61.7 21.2 all-gather.5
  86.0 19.6 reduce-scatter.37
  108.5 19.6 reduce-scatter.33
  131.1 19.6 reduce-scatter.35
  153.1 41.2 reduce-scatter.25
  197.0 41.2 reduce-scatter.17
  240.8 41.2 reduce-scatter.19
  286.6 21.0 all-gather.11
  309.7 21.0 all-gather.13
  332.9 21.0 all-gather.7
  356.2 31.8 reduce-scatter.27
  390.4 31.8 reduce-scatter.21
  424.9 9.9 reduce-scatter.29
  437.5 9.9 reduce-scatter.23
  450.1 9.9 reduce-scatter.31
  462.4 86.9 all-reduce.11
  552.9 39.1 all-reduce.13
  597.0 75.6 all-reduce.9
where the time goes:
time: 691 us; the launch traced here: 690 us
  waiting for transfers between devices  448 us (65%)
  matrix products  122 us (18%)
  blocking collectives  87.7 us (13%)
  between operations  14.4 us (2%)
  local copies, waits for them, and re-layouts  13.6 us (2%)
    psum x1, waiting for transfers between devices, on_device(): lax.psum((grad_gate_reduce, grad_up_reduce), ('gx', 'gz'))  80.6 us
    psum x1, waiting for transfers between devices, on_device(): down_lin, down_lowsum = lax.psum((down_lin, down_lowsum), 'gz')  64.4 us
    dot_general x8, matrix products, contract_last(): lax.dot_general(left, right, (((1,), (1,)), ((), ())), preferred_element_...  43.7 us
    reduce_scatter x1, waiting for transfers between devices, on_device(): lax.psum_scatter(part_hidden_grad, 'gy', scatter_dimension=0, tiled=True)  42.8 us
    reduce_scatter x1, waiting for transfers between devices, on_device(): lax.psum_scatter(part_gate, 'gy', scatter_dimension=0, tiled=True)  42.3 us
    reduce_scatter x1, waiting for transfers between devices, on_device(): lax.psum_scatter(part_up, 'gy', scatter_dimension=0, tiled=True)  42.3 us
    reduce_scatter x1, waiting for transfers between devices, on_device(): lax.psum_scatter(part_down, 'gx', scatter_dimension=0, tiled=True)  34.2 us
    dot_general x3, matrix products, tile_square(): jnp.dot(reduce_in, expand_out, preferred_element_type=jnp.float32)  24.6 us
  transfers between devices with their start and end apart: 19, of which 16 were waited for; matrix products, arithmetic and copies ran while one was open for 16% of the time, Pallas kernels for 0%

commit v1 on v0

--- a/solution.py
+++ b/solution.py
@@ -152,7 +152,9 @@
     token_share = share_rows(tokens, share_count)
     grad_gate_reduce = contract_first(token_share, gate_back)
     grad_up_reduce = contract_first(token_share, up_back)
-    grad_gate_reduce, grad_up_reduce = lax.psum((grad_gate_reduce, grad_up_reduce), ("gx", "gz"))
+    grad_gate_reduce, grad_up_reduce = lax.psum(
+        lax.psum((grad_gate_reduce, grad_up_reduce), "gx"), "gz"
+    )
     return (
         output,
         grad_tokens,

time: 691 us -> 728 us (1.054)
  waiting for transfers between devices: 448 us -> 489 us
    psum x1, waiting for transfers between devices: 64.4 us -> 89.7 us  [on_device(): down_lin, down_lowsum = lax.psum((down_lin, down_lowsum), 'gz')]
    all_gather x1, waiting for transfers between devices: 20.5 us -> 0.02 us  [on_device(): all_tokens = lax.all_gather(tokens, 'gx', axis=0, tiled=True)]
    reduce_scatter x1, waiting for transfers between devices: 14.4 us -> 34 us  [on_device(): lax.psum_scatter(part_input, 'gx', scatter_dimension=0, tiled=True)]
    reduce_scatter x1, waiting for transfers between devices: 0.01 us -> 12.6 us  [on_device(): lax.psum_scatter(part_gate_back, 'gx', scatter_dimension=0, tiled=True)]
    all_gather x1, waiting for transfers between devices: 12.1 us -> 20.3 us  [on_device(): lax.all_gather(up_delta, 'gy', axis=0, tiled=True)]
    all_gather x1, waiting for transfers between devices: 11.6 us -> 19.7 us  [on_device(): all_hidden = lax.all_gather(hidden, 'gy', axis=0, tiled=True)]
    psum x1 -> x2, waiting for transfers between devices: 80.6 us -> 74.8 us  [the longest x1 74.8 us: on_device(): lax.psum((grad_down_magnitude, grad_down_expand), ('gx', 'gz'))]
  transfers between devices with their start and end apart: 19 -> 20, of which waited for: 16 -> 16; matrix products, arithmetic and copies ran while one was open for 16% -> 16% of each run, Pallas kernels for 0% -> 0%
where the time goes in v1:
time: 728 us; the launch traced here: 727 us
  waiting for transfers between devices  489 us (67%)
  matrix products  119 us (16%)
  blocking collectives  87 us (12%)
  between operations  14.8 us (2%)
  local copies, waits for them, and re-layouts  13.7 us (2%)
    psum x1, waiting for transfers between devices, on_device(): down_lin, down_lowsum = lax.psum((down_lin, down_lowsum), 'gz')  89.7 us
    psum x1, waiting for transfers between devices, on_device(): lax.psum((grad_down_magnitude, grad_down_expand), ('gx', 'gz'))  74.8 us
    reduce_scatter x1, waiting for transfers between devices, on_device(): lax.psum_scatter(part_hidden_grad, 'gy', scatter_dimension=0, tiled=True)  42.8 us
    reduce_scatter x1, waiting for transfers between devices, on_device(): lax.psum_scatter(part_gate, 'gy', scatter_dimension=0, tiled=True)  42.3 us
    reduce_scatter x1, waiting for transfers between devices, on_device(): lax.psum_scatter(part_up, 'gy', scatter_dimension=0, tiled=True)  41.4 us
    dot_general x8, matrix products, contract_last(): lax.dot_general(left, right, (((1,), (1,)), ((), ())), preferred_element_...  39.5 us
    reduce_scatter x1, waiting for transfers between devices, on_device(): lax.psum_scatter(part_input, 'gx', scatter_dimension=0, tiled=True)  34 us
    reduce_scatter x1, waiting for transfers between devices, on_device(): lax.psum_scatter(part_down, 'gx', scatter_dimension=0, tiled=True)  29.7 us
  transfers between devices with their start and end apart: 20, of which 16 were waited for; matrix products, arithmetic and copies ran while one was open for 16% of the time, Pallas kernels for 0%

profile of v1, /device:TPU:0, one launch (start us, length us, event | category | flops | bytes accessed | tf_op | source)
XLA Modules:
  0.0 727.0 jit_solution(5774637096116925505)
XLA Ops:
  8.0 9.5 %multiply_reduce_fusion = f32[2048]{0:T(1024)S(1)} fusion(bf16[3584,2048]{1,0:T(8,128)(2,1)} %param.18, bf16[3584,32]{0,1:T(8,128)(2,1)} %param.25, bf16[32,2048]{1,0:T(8,128)(2,1)} %param.26), kind=kOutput, calls=%fused_computation | convolution fusion | flops 499120128 | bytes 15048704 | tf_op jit(solution)/shard_map/dot_general | solution.py:10
  17.5 23.8 %psum.137 = f32[2048]{0:T(1024)S(1)} all-reduce(f32[2048]{0:T(1024)S(1)} %multiply_reduce_fusion), channel_id=1, replica_groups=mesh['gx'=2,'gy'=4,'gz'=4] {'gx','gz'}, use_global_device_ids=true, to_apply=%region_13.0 | all-reduce | flops 2048 | bytes 16384 | tf_op jit(solution)/shard_map/psum | solution.py:52
  47.2 13.8 %all-gather.10.cloned.1.call-done = bf16[256,2048]{1,0:T(8,128)(2,1)} async-done(((bf16[128,2048]{1,0:T(8,128)(2,1)}), bf16[256,2048]{1,0:T(8,128)(2,1)}) %all-gather.10.cloned.1.call-update) | async-done | bytes 1048592 | tf_op jit(solution)/shard_map/all_gather | solution.py:101
  63.3 11.4 %fusion.37 = f32[256,3584]{1,0:T(8,128)} fusion(bf16[256,2048]{1,0:T(8,128)(2,1)} %all-gather.10.cloned.1.call-done, bf16[3584,2048]{1,0:T(8,128)(2,1)} %param.18), kind=kOutput, calls=%fused_computation.60 | convolution fusion | flops 3758096384 | bytes 19398656 | tf_op jit(solution)/shard_map/dot_general | solution.py:21
  108.6 11.0 %all-reduce.3 = (f32[3584]{0:T(1024)S(1)}, f32[3584]{0:T(1024)S(1)}) all-reduce(f32[3584]{0:T(1024)S(1)} %multiply_reduce_fusion.1, f32[3584]{0:T(1024)S(1)} %multiply_reduce_fusion.2), channel_id=1, replica_groups=mesh['gx'=2,'gy'=4,'gz'=4] {'gy'}, use_global_device_ids=true, to_apply=%region_7.0 | all-reduce | flops 7168 | bytes 57344 | tf_op jit(solution)/shard_map/psum | solution.py:65
  129.5 42.8 %reduce-scatter.26.cloned.1.call-done = f32[64,3584]{1,0:T(8,128)} async-done(((f32[256,3584]{1,0:T(8,128)}), f32[64,3584]{1,0:T(8,128)}) %reduce-scatter.26.cloned.1.call-update) | async-done | bytes 917520 | tf_op jit(solution)/shard_map/reduce_scatter | solution.py:105
  173.8 42.3 %reduce-scatter.18.cloned.1.call-done = f32[64,3584]{1,0:T(8,128)} async-done(((f32[256,3584]{1,0:T(8,128)}), f32[64,3584]{1,0:T(8,128)}) %reduce-scatter.18.cloned.1.call-update) | async-done | bytes 917520 | tf_op jit(solution)/shard_map/reduce_scatter | solution.py:60
  218.6 41.4 %reduce-scatter.20.cloned.1.call-done = f32[64,3584]{1,0:T(8,128)} async-done(((f32[256,3584]{1,0:T(8,128)}), f32[64,3584]{1,0:T(8,128)}) %reduce-scatter.20.cloned.1.call-update) | async-done | bytes 917520 | tf_op jit(solution)/shard_map/reduce_scatter | solution.py:61
  265.4 19.7 %all-gather.8.cloned.1.call-done = bf16[256,3584]{1,0:T(8,128)(2,1)} async-done(((bf16[64,3584]{1,0:T(8,128)(2,1)}), bf16[256,3584]{1,0:T(8,128)(2,1)}) %all-gather.8.cloned.1.call-update) | async-done | bytes 1835024 | tf_op jit(solution)/shard_map/all_gather | solution.py:79
  287.9 20.3 %all-gather.14.cloned.1.call-done = bf16[256,3584]{1,0:T(8,128)(2,1)} async-done(((bf16[64,3584]{1,0:T(8,128)(2,1)}), bf16[256,3584]{1,0:T(8,128)(2,1)}) %all-gather.14.cloned.1.call-update) | async-done | bytes 1835024 | tf_op jit(solution)/shard_map/all_gather | solution.py:134
  311.0 20.5 %all-gather.12.cloned.1.call-done = bf16[256,3584]{1,0:T(8,128)(2,1)} async-done(((bf16[64,3584]{1,0:T(8,128)(2,1)}), bf16[256,3584]{1,0:T(8,128)(2,1)}) %all-gather.12.cloned.1.call-update) | async-done | bytes 1835024 | tf_op jit(solution)/shard_map/all_gather | solution.py:133
  334.3 9.8 %reduce-scatter.24.cloned.1.call-done = f32[128,32]{0,1:T(8,128)} async-done(((f32[256,32]{0,1:T(8,128)}), f32[128,32]{0,1:T(8,128)}) %reduce-scatter.24.cloned.1.call-update) | async-done | bytes 16400 | tf_op jit(solution)/shard_map/reduce_scatter | solution.py:84
  344.1 12.8 %reduce-scatter.32.cloned.1.call-done = f32[128,32]{0,1:T(8,128)} async-done(((f32[256,32]{0,1:T(8,128)}), f32[128,32]{0,1:T(8,128)}) %reduce-scatter.32.cloned.1.call-update) | async-done | bytes 16400 | tf_op jit(solution)/shard_map/reduce_scatter | solution.py:142
  356.9 12.6 %reduce-scatter.30.cloned.1.call-done = f32[128,32]{0,1:T(8,128)} async-done(((f32[256,32]{0,1:T(8,128)}), f32[128,32]{0,1:T(8,128)}) %reduce-scatter.30.cloned.1.call-update) | async-done | bytes 16400 | tf_op jit(solution)/shard_map/reduce_scatter | solution.py:141
  369.5 19.9 %all-reduce = (bf16[128,32]{0,1:T(8,128)(2,1)S(1)}, bf16[128,32]{0,1:T(8,128)(2,1)S(1)}, bf16[128,32]{0,1:T(8,128)(2,1)S(1)}) all-reduce(f32[128,32]{0,1:T(8,128)} %reduce-scatter.24.cloned.1.call-done, f32[128,32]{0,1:T(8,128)} %reduce-scatter.30.cloned.1.call-done, ...), channel_id=1, replica_groups=mesh['gx'=2,'gy'=4,'gz'=4] {'gz'}, use_global_device_ids=true, to_apply=%region_11.0 | all-reduce | flops 12288 | bytes 73728 | tf_op jit(solution)/shard_map/psum | solution.py:86
  391.6 11.3 %fusion.35 = f32[256,2048]{1,0:T(8,128)} fusion(bf16[256,3584]{1,0:T(8,128)(2,1)} %all-gather.8.cloned.1.call-done, bf16[3584,2048]{1,0:T(8,128)(2,1)} %param.18), kind=kOutput, calls=%fused_computation.58 | convolution fusion | flops 3758096384 | bytes 18612224 | tf_op jit(solution)/shard_map/dot_general | solution.py:80
  410.4 11.2 %convolution_add_fusion.3 = f32[256,2048]{1,0:T(8,128)} fusion(f32[256,2048]{1,0:T(8,128)S(1)} %fusion.39, bf16[256,3584]{1,0:T(8,128)(2,1)} %all-gather.14.cloned.1.call-done, bf16[2048,3584]{1,0:T(8,128)(2,1)} %param.17), kind=kOutput, calls=%fused_computation.8 | convolution fusion | flops 3758620672 | bytes 20709376 | tf_op jit(solution)/shard_map/dot_general | solution.py:21
  421.7 29.7 %reduce-scatter.22.cloned.1.call-done = f32[128,2048]{1,0:T(8,128)} async-done(((f32[256,2048]{1,0:T(8,128)}), f32[128,2048]{1,0:T(8,128)}) %reduce-scatter.22.cloned.1.call-update) | async-done | bytes 1048592 | tf_op jit(solution)/shard_map/reduce_scatter | solution.py:83
  451.4 34.0 %reduce-scatter.28.cloned.1.call-done = f32[128,2048]{1,0:T(8,128)} async-done(((f32[256,2048]{1,0:T(8,128)}), f32[128,2048]{1,0:T(8,128)}) %reduce-scatter.28.cloned.1.call-update) | async-done | bytes 1048592 | tf_op jit(solution)/shard_map/reduce_scatter | solution.py:140
  488.6 11.9 %all-reduce.2 = (f32[3584]{0:T(1024)}, f32[3584]{0:T(1024)}) all-reduce(f32[3584]{0:T(1024)S(1)} %get-tuple-element.34, f32[3584]{0:T(1024)S(1)} %get-tuple-element.35), channel_id=1, replica_groups=mesh['gx'=2,'gy'=4,'gz'=4] {'gy'}, use_global_device_ids=true, to_apply=%region_26.0 | all-reduce | flops 7168 | bytes 57344 | tf_op jit(solution)/shard_map/psum | solution.py:121
  502.4 89.7 %all-reduce.13.cloned.1.call-done = (f32[128,2048]{1,0:T(8,128)}, f32[128,2048]{1,0:T(8,128)}, f32[2048,32]{0,1:T(8,128)}, f32[2048,32]{0,1:T(8,128)}) async-done(((f32[128,2048]{1,0:T(8,128)}, f32[128,2048]{1,0:T(8,128)}, f32[2048,32]{0,1:T(8,128)}, f32[2048,32]{0,1:T(8,128)}), (f32[128,2048]{1,0:T(8,128)}, f32[128,2048]{1,0:T(8,128)}, f32[2048,32]{0,1:T(8,128)}, ...) | async-done | bytes 2621456 | tf_op jit(solution)/shard_map/psum | solution.py:86
  594.5 20.4 %psum.151 = f32[2048]{0:T(1024)} all-reduce(f32[2048]{0:T(1024)S(1)} %fusion.17), channel_id=1, replica_groups=mesh['gx'=2,'gy'=4,'gz'=4] {'gx','gz'}, use_global_device_ids=true, to_apply=%region_35.0 | all-reduce | flops 2048 | bytes 16384 | tf_op jit(solution)/shard_map/psum | solution.py:98
  617.5 17.4 %all-reduce.15.cloned.1.call-done = (f32[32,3584]{1,0:T(8,128)}, f32[32,3584]{1,0:T(8,128)}, f32[3584,32]{0,1:T(8,128)}) async-done(((f32[32,3584]{1,0:T(8,128)}, f32[32,3584]{1,0:T(8,128)}, f32[3584,32]{0,1:T(8,128)}), (f32[32,3584]{1,0:T(8,128)}, f32[32,3584]{1,0:T(8,128)}, f32[3584,32]{0,1:T(8,128)})) %all-reduce.15.cloned.1.call-update) | async-done | bytes 1376272 | tf_op jit(solution)/shard_map/psum | solution.py:121
  634.9 74.8 %all-reduce.11.cloned.1.call-done = f32[32,2048]{1,0:T(8,128)} async-done(((f32[32,2048]{1,0:T(8,128)}), f32[32,2048]{1,0:T(8,128)}) %all-reduce.11.cloned.1.call-update) | async-done | bytes 262160 | tf_op jit(solution)/shard_map/psum | solution.py:98
  (128 shorter events, 100.3 us)
Async XLA Ops:
  7.2 93.8 %copy-start = (bf16[32,3584]{1,0:T(8,128)(2,1)S(1)}, bf16[32,3584]{1,0:T(8,128)(2,1)}, u32[]{:S(2)}) copy-start(bf16[32,3584]{1,0:T(8,128)(2,1)} %param.23) | copy-start | bytes 688132
  7.2 35.1 %all-gather.6.cloned.1.call-start = ((), (), s32[]{:S(2)}) async-start(), calls=%async_computation.11 | async-start | bytes 1572864 | tf_op jit(solution)/shard_map/all_gather | solution.py:54
  8.0 53.0 %all-gather.10.cloned.1.call-start = ((), (), s32[]{:S(2)}) async-start(), calls=%async_computation.17 | async-start | bytes 1572864 | tf_op jit(solution)/shard_map/all_gather | solution.py:101
  42.3 78.0 %reduce-scatter.36.cloned.1.call-start = ((), (), s32[]{:S(2)}) async-start(), calls=%async_computation.26 | async-start | bytes 163840
  44.7 77.0 %reduce-scatter.34.cloned.1.call-start = ((), (), s32[]{:S(2)}) async-start(), calls=%async_computation.25 | async-start | bytes 163840
  47.1 81.6 %reduce-scatter.38.cloned.1.call-start = ((), (), s32[]{:S(2)}) async-start(), calls=%async_computation.27 | async-start | bytes 163840
  63.3 109.1 %reduce-scatter.26.cloned.1.call-start = ((), (), s32[]{:S(2)}) async-start(), calls=%async_computation.18 | async-start | bytes 4587520 | tf_op jit(solution)/shard_map/reduce_scatter | solution.py:105
  74.7 141.4 %reduce-scatter.18.cloned.1.call-start = ((), (), s32[]{:S(2)}) async-start(), calls=%async_computation.12 | async-start | bytes 4587520 | tf_op jit(solution)/shard_map/reduce_scatter | solution.py:60
  84.0 176.0 %reduce-scatter.20.cloned.1.call-start = ((), (), s32[]{:S(2)}) async-start(), calls=%async_computation.13 | async-start | bytes 4587520 | tf_op jit(solution)/shard_map/reduce_scatter | solution.py:61
  93.3 191.8 %all-gather.8.cloned.1.call-start = ((), (), s32[]{:S(2)}) async-start(), calls=%async_computation.14 | async-start | bytes 2293760 | tf_op jit(solution)/shard_map/all_gather | solution.py:79
  108.6 280.8 %copy-start.7 = (bf16[128,2048]{1,0:T(8,128)(2,1)S(1)}, bf16[128,2048]{1,0:T(8,128)(2,1)}, u32[]{:S(2)}) copy-start(bf16[128,2048]{1,0:T(8,128)(2,1)} %param.14) | copy-start | bytes 1572868
  263.9 44.4 %all-gather.14.cloned.1.call-start = ((), (), s32[]{:S(2)}) async-start(), calls=%async_computation.20 | async-start | bytes 2293760 | tf_op jit(solution)/shard_map/all_gather | solution.py:134
  264.4 67.0 %all-gather.12.cloned.1.call-start = ((), (), s32[]{:S(2)}) async-start(), calls=%async_computation.19 | async-start | bytes 2293760 | tf_op jit(solution)/shard_map/all_gather | solution.py:133
  265.3 78.7 %reduce-scatter.24.cloned.1.call-start = ((), (), s32[]{:S(2)}) async-start(), calls=%async_computation.16 | async-start | bytes 49152 | tf_op jit(solution)/shard_map/reduce_scatter | solution.py:84
  287.9 69.0 %reduce-scatter.32.cloned.1.call-start = ((), (), s32[]{:S(2)}) async-start(), calls=%async_computation.23 | async-start | bytes 49152 | tf_op jit(solution)/shard_map/reduce_scatter | solution.py:142
  311.0 58.5 %reduce-scatter.30.cloned.1.call-start = ((), (), s32[]{:S(2)}) async-start(), calls=%async_computation.22 | async-start | bytes 49152 | tf_op jit(solution)/shard_map/reduce_scatter | solution.py:141
  334.2 87.4 %all-reduce.17.cloned.1.call-start = ((), (), s32[]{:S(2)}) async-start(), calls=%async_computation.30 | async-start | bytes 1048576 | tf_op jit(solution)/shard_map/psum | solution.py:156
  391.3 60.1 %reduce-scatter.22.cloned.1.call-start = ((), (), s32[]{:S(2)}) async-start(), calls=%async_computation.15 | async-start | bytes 3145728 | tf_op jit(solution)/shard_map/reduce_scatter | solution.py:83
  402.9 82.5 %reduce-scatter.28.cloned.1.call-start = ((), (), s32[]{:S(2)}) async-start(), calls=%async_computation.21 | async-start | bytes 3145728 | tf_op jit(solution)/shard_map/reduce_scatter | solution.py:140
  410.4 181.7 %copy-start.14 = (bf16[32,2048]{1,0:T(8,128)(2,1)S(1)}, bf16[32,2048]{1,0:T(8,128)(2,1)}, u32[]{:S(2)}) copy-start(bf16[32,2048]{1,0:T(8,128)(2,1)} %param.26) | copy-start | bytes 393220
  421.6 194.8 %copy-start.12 = (bf16[2048,32]{0,1:T(8,128)(2,1)S(1)}, bf16[2048,32]{0,1:T(8,128)(2,1)}, u32[]{:S(2)}) copy-start(bf16[2048,32]{0,1:T(8,128)(2,1)} %param.22) | copy-start | bytes 393220
  421.6 170.5 %all-reduce.13.cloned.1.call-start = ((), (), s32[]{:S(2)}) async-start(), calls=%async_computation.28 | async-start | bytes 5242880 | tf_op jit(solution)/shard_map/psum | solution.py:86
  485.4 149.5 %all-reduce.15.cloned.1.call-start = ((), (), s32[]{:S(2)}) async-start(), calls=%async_computation.29 | async-start | bytes 2752512 | tf_op jit(solution)/shard_map/psum | solution.py:121
  488.4 221.3 %all-reduce.11.cloned.1.call-start = ((), (), s32[]{:S(2)}) async-start(), calls=%async_computation.24 | async-start | bytes 524288 | tf_op jit(solution)/shard_map/psum | solution.py:98
  (17 other events, 793.3 us)
Sparse Core Ops, SparseCore 0:
  9.5 24.4 all-gather.5
  42.4 18.5 all-gather.9
  64.0 19.6 reduce-scatter.35
  86.5 19.6 reduce-scatter.33
  109.0 19.6 reduce-scatter.37
  131.1 41.2 reduce-scatter.25
  174.9 41.2 reduce-scatter.17
  218.7 41.2 reduce-scatter.19
  264.0 21.0 all-gather.7
  287.1 21.0 all-gather.13
  310.3 21.0 all-gather.11
  334.1 9.9 reduce-scatter.23
  346.8 9.9 reduce-scatter.31
  359.5 9.9 reduce-scatter.29
  391.4 25.8 all-reduce.16
  419.4 31.8 reduce-scatter.21
  453.5 31.8 reduce-scatter.27
  487.9 104.1 all-reduce.12
  595.8 39.1 all-reduce.14
  638.7 71.0 all-reduce.10
